TPU v7x, 256 devices: a whole 4x4x8 slice. The times are simulated.
256 devices in a mesh: elem: 64 (over y, z, core), snap: 4 (over x).
Axes of the slice: x: 4, y: 4, z: 8, core: 2. Of those that a mesh axis runs over, the one named last changes fastest.
Arguments:
- node_basis: bfloat16 [65536, 1536], P('elem'), may hold values from -0.25 to 0.25
- stiff_terms: bfloat16 [16, 24, 24], replicated, may hold values from -1.25 to 1.25
- reduced_coords: bfloat16 [512, 32], P(None, 'snap'), may hold values from -6 to 6
- sample_list: int32 [512], replicated, may hold values from 0 to 2047, as said below
- connectivity: int32 [2048, 8], replicated, may hold values from -1 to 65535, as said below
- node_slot: int32 [65536], replicated, may hold values from 0 to 65535, as said below
- elem_device: int32 [512], replicated, may hold values from 0 to 63, as said below
Outputs:
- ortho_panel: float32 [1024, 512, 512], P('elem', 'snap')
- triangle_factor: float32 [512, 512], P('elem')
Inputs may be any that keep to these rules, and one draw needn't show every extreme that they name: `sample_list`: distinct element ids. `connectivity`: each element lists 4, 6 or 8 live nodes first and -1 after them; the live nodes of one element are owned by distinct indices of elem (owner = node_slot // 1024); for every index d of elem and every owner o, at most 2 sampled elements computed on d have a live node owned by o, and some pair (d, o) reaches 2. `node_slot`: a permutation. `elem_device`: each index of elem computes at most 16 sampled elements; some index computes exactly 16.
All inputs are finite; a program needn't handle non-finite values.
Results may differ from a plain program's by a relative error of at most 0.0056.
Values may be sent and summed in bfloat16 or wider, within the bound.
A program may use at most 64 MiB of HBM per device.

v0:
```python
import jax
import jax.numpy as jnp
from jax import lax
from jax.sharding import PartitionSpec as P

MODES = 512
ENODES = 8
NDOF = 3


def shards(
    node_basis, stiff_terms, reduced_coords, sample_list, connectivity, node_slot, elem_device
):
    devices = lax.axis_size("elem")
    elem_rank = lax.axis_index("elem")
    node_rows = node_basis.shape[0]
    sampled = sample_list.shape[0]
    capacity = 2 * sampled // devices
    pair_bound = (capacity * ENODES + devices - 1) // devices
    node_ids = connectivity[sample_list]
    live_nodes = node_ids >= 0
    stored_rows = jnp.where(live_nodes, node_slot[jnp.maximum(node_ids, 0)], 0)
    owners = stored_rows // node_rows
    local_rows = stored_rows % node_rows
    position_ids = jnp.arange(sampled, dtype=jnp.int32)
    earlier = position_ids[None, :] < position_ids[:, None]
    same_device = elem_device[None, :] == elem_device[:, None]
    in_group = earlier & same_device
    slot_ids = jnp.sum(in_group.astype(jnp.int32), axis=1)
    owner_ids = jnp.arange(devices, dtype=jnp.int32)
    owned_mask = jnp.any(live_nodes[:, :, None] & (owners[:, :, None] == owner_ids), axis=1).astype(
        jnp.float32
    )
    ranks_by_owner = jnp.dot(
        in_group.astype(jnp.float32), owned_mask, precision=lax.Precision.HIGHEST
    ).astype(jnp.int32)
    peer_ranks = jnp.take_along_axis(ranks_by_owner, owners, axis=1)
    sending = live_nodes & (owners == elem_rank)
    target = jnp.where(sending, elem_device[:, None], devices)
    row_table = (
        jnp.full((devices, pair_bound), -1, jnp.int32)
        .at[target, peer_ranks]
        .set(local_rows, mode="drop")
    )
    send_rows = node_basis[jnp.maximum(row_table, 0)]
    outgoing = jnp.where((row_table >= 0)[:, :, None], send_rows, jnp.zeros((), jnp.bfloat16))
    incoming = lax.all_to_all(outgoing, "elem", split_axis=0, concat_axis=0, tiled=True)
    at_device = elem_device == elem_rank
    slot_index = jnp.where(at_device, slot_ids, capacity)
    slot_elem = (
        jnp.full((capacity,), sampled, jnp.int32).at[slot_index].set(position_ids, mode="drop")
    )
    slot_live = slot_elem < sampled
    picked = jnp.minimum(slot_elem, sampled - 1)
    slot_rows = incoming[owners[picked], jnp.minimum(peer_ranks[picked], pair_bound - 1)]
    slot_mask = live_nodes[picked] & slot_live[:, None]
    local_basis = jnp.where(slot_mask[:, :, None], slot_rows, jnp.zeros((), jnp.bfloat16))
    element_basis = local_basis.reshape(capacity, ENODES * NDOF, MODES)
    displaced = jnp.einsum(
        "ekm,ms->eks", element_basis, reduced_coords, preferred_element_type=jnp.float32
    ).astype(jnp.bfloat16)
    forces = jnp.einsum(
        "tkl,els->ekst", stiff_terms, displaced, preferred_element_type=jnp.float32
    ).astype(jnp.bfloat16)
    forces = forces.reshape(capacity, ENODES * NDOF, -1)
    projected = jnp.einsum(
        "ekm,ekc->emc", element_basis, forces, preferred_element_type=jnp.float32
    ).astype(jnp.bfloat16)
    banded = lax.all_to_all(projected, "snap", split_axis=1, concat_axis=2, tiled=True)
    band_rows = banded.reshape(-1, banded.shape[2])
    columns = band_rows.shape[1]
    total_rows = sampled * MODES
    partial_gram = lax.dot_general(
        band_rows, band_rows, (((0,), (0,)), ((), ())), preferred_element_type=jnp.float32
    )
    gram_matrix = lax.psum(partial_gram, ("elem", "snap"))
    gram_matrix = gram_matrix / total_rows
    lower_factor = jnp.linalg.cholesky(gram_matrix)
    identity_matrix = jnp.eye(columns, dtype=jnp.float32)
    lower_inverse = jax.scipy.linalg.solve_triangular(lower_factor, identity_matrix, lower=True)
    ortho_rows = lax.dot_general(
        band_rows.astype(jnp.float32),
        lower_inverse,
        (((1,), (1,)), ((), ())),
        precision=lax.Precision.HIGHEST,
        preferred_element_type=jnp.float32,
    )
    share = columns // devices
    upper_rows = lax.dynamic_slice_in_dim(lower_factor.T, elem_rank * share, share, 0)
    return (ortho_rows.reshape(banded.shape), upper_rows)


def solution(mesh):
    placed = (P("elem", None), P(), P(None, "snap"), P(), P(), P(), P())
    return jax.shard_map(
        shards,
        mesh=mesh,
        in_specs=placed,
        out_specs=(P("elem", "snap", None), P("elem", None)),
        check_vma=False,
    )
```

profile of v0, /device:TPU:2, one launch (start us, length us, event | category | flops | bytes accessed | tf_op | source)
XLA Modules:
  0.0 630.0 jit_solution(7660797386319666554)
XLA Ops:
  10.3 2.9 gather_fusion
  15.9 23.0 %gather_fusion.2 = s32[4096]{0:T(1024)S(1)} fusion(s32[65536]{0:T(1024)S(1)} %copy-done.1, s32[4096]{0:T(1024)S(1)} %broadcast_clamp_fusion), kind=kCustom, calls=%fused_computation.2 | custom fusion | bytes 49152 | tf_op jit(solution)/shard_map/gather | solution.py:22
  48.0 33.0 %gather_fusion.7 = s32[4096]{0:T(1024)S(1)} fusion(s32[512,64]{0,1:T(8,128)S(1)} %convolution_convert_fusion.2, s32[4096]{0:T(1024)S(1)} %reshape.363), kind=kCustom, calls=%fused_computation.7 | custom fusion | bytes 65536 | tf_op jit(solution)/shard_map/jit(take_along_axis)/gather | solution.py:37
  88.4 15.5 %scatter_custom_fusion.1 = s32[128]{0:T(128)S(1)} fusion(s32[4096]{0:T(1024)S(1)} %reshape.377, s32[4096]{0:T(1024)S(1)} %reshape.379, s32[]{:T(128)} %constant.211.clone.1), kind=kCustom, calls=%fused_computation.155 | custom fusion | bytes 516
  109.7 12.1 %all-to-all-start = ((bf16[64,2,1536]{2,1,0:T(2,128)(2,1)}), bf16[64,2,1536]{2,1,0:T(2,128)(2,1)S(1)}, u32[]{:S(2)}, u32[]{:S(2)}) async-start(bf16[64,2,1536]{2,1,0:T(2,128)(2,1)} %broadcast_select_fusion), calls=%async_computation | async-start | bytes 786432 | tf_op jit(solution)/shard_map/all_to_all | solution.py:47
  124.7 3.2 scatter_custom_fusion
  151.1 29.8 %all_to_all.20 = bf16[16,512,128]{2,0,1:T(8,128)(2,1)} all-to-all(bf16[16,512,128]{2,0,1:T(8,128)(2,1)S(1)} %copy.125), channel_id=1, replica_groups=mesh['elem'=64,'snap'=4] {'snap'}, dimensions={1} | all-to-all | bytes 4194304 | tf_op jit(solution)/shard_map/all_to_all | solution.py:69
  180.9 5.1 copy.126
  186.0 4.5 fusion
  192.4 4.5 copy.127
  197.0 4.3 dot_general.24
  201.3 248.6 %all-reduce.3.cloned.1.call-done = f32[512,512]{0,1:T(8,128)} async-done(((f32[512,512]{0,1:T(8,128)}), f32[512,512]{0,1:T(8,128)}) %all-reduce.3.cloned.1.call-update) | async-done | bytes 1048592 | tf_op jit(solution)/shard_map/psum | solution.py:76
  457.4 11.7 %cholesky.104 = f32[128,128]{1,0:T(8,128)S(1)} custom-call(f32[128,128]{1,0:T(8,128)S(1)} %cholesky.266), custom_call_target="Cholesky" | custom-call | tf_op jit(solution)/shard_map/jit(cholesky)/cholesky | solution.py:78
  469.7 9.8 %custom-call.31 = f32[1,128,128]{1,2,0:T(8,128)S(1)} custom-call(f32[1,128,128]{2,1,0:T(8,128)S(1)} %get-tuple-element.47), custom_call_target="InvertDiagBlocksLowerTriangular" | custom-call | tf_op jit(solution)/shard_map/jit(cholesky)/cholesky | solution.py:78
  484.0 11.7 %cholesky.217 = f32[128,128]{1,0:T(8,128)S(1)} custom-call(f32[128,128]{1,0:T(8,128)S(1)} %cholesky.270), custom_call_target="Cholesky" | custom-call | tf_op jit(solution)/shard_map/jit(cholesky)/cholesky | solution.py:78
  499.0 10.2 %custom-call.32 = f32[1,128,128]{1,2,0:T(8,128)S(1)} custom-call(f32[1,128,128]{2,1,0:T(8,128)S(1)} %get-tuple-element.44), custom_call_target="InvertDiagBlocksLowerTriangular" | custom-call | tf_op jit(solution)/shard_map/jit(cholesky)/cholesky | solution.py:78
  512.5 11.7 %cholesky.238 = f32[128,128]{1,0:T(8,128)S(1)} custom-call(f32[128,128]{1,0:T(8,128)S(1)} %cholesky.275), custom_call_target="Cholesky" | custom-call | tf_op jit(solution)/shard_map/jit(cholesky)/cholesky | solution.py:78
  525.5 9.8 %custom-call.33 = f32[1,128,128]{1,2,0:T(8,128)S(1)} custom-call(f32[1,128,128]{2,1,0:T(8,128)S(1)} %get-tuple-element.41), custom_call_target="InvertDiagBlocksLowerTriangular" | custom-call | tf_op jit(solution)/shard_map/jit(cholesky)/cholesky | solution.py:78
  537.6 11.9 %cholesky.255 = f32[128,128]{1,0:T(8,128)S(1)} custom-call(f32[128,128]{1,0:T(8,128)S(1)} %convolution_subtract_fusion.5), custom_call_target="Cholesky" | custom-call | tf_op jit(solution)/shard_map/jit(cholesky)/cholesky | solution.py:78
  557.2 13.5 %while.1 = (s32[]{:T(128)}, f32[512,512]{1,0:T(8,128)}, s32[4,2]{0,1:T(2,128)S(1)}, f32[4,128,128]{2,1,0:T(8,128)}, s32[]{:T(128)}) while((s32[]{:T(128)}, f32[512,512]{1,0:T(8,128)}, s32[4,2]{0,1:T(2,128)S(1)}, f32[4,128,128]{2,1,0:T(8,128)}, s32[]{:T(128)}) %tuple.39), condition=%wide.while_cond, body=%wide.while_body.sunk | while | flops 2 | bytes 132205 | solution.py:80
  557.8 2.8 bitcast_dynamic-update-slice_fusion.2
  561.2 2.8 bitcast_dynamic-update-slice_fusion.2
  570.7 40.1 %custom-call.34 = f32[4,128,128]{1,2,0:T(8,128)S(1)} custom-call(f32[4,128,128]{2,1,0:T(8,128)} %get-tuple-element.9), custom_call_target="InvertDiagBlocksLowerTriangular" | custom-call | tf_op jit(solution)/shard_map/jit(_solve_triangular)/triangular_solve | solution.py:80
  617.9 5.1 fusion.4
  (137 shorter events, 98.7 us)
Async XLA Ops:
  7.2 97.9 %copy-start = (bf16[1024,1536]{1,0:T(8,128)(2,1)S(1)}, bf16[1024,1536]{1,0:T(8,128)(2,1)}, u32[]{:S(2)}) copy-start(bf16[1024,1536]{1,0:T(8,128)(2,1)} %param.7) | copy-start | bytes 9437188
  8.0 7.9 %copy-start.1 = (s32[65536]{0:T(1024)S(1)}, s32[65536]{0:T(1024)}, u32[]{:S(2)}) copy-start(s32[65536]{0:T(1024)} %param.12) | copy-start | bytes 786436
  39.0 8.6 %copy-start.8 = (s32[512]{0:T(512)S(1)}, s32[512]{0:T(512)}, u32[]{:S(2)}) copy-start(s32[512]{0:T(512)} %param.13) | copy-start | bytes 6148
  40.0 1.9 copy-start.5
  41.9 40.0 %copy-start.6 = (pred[512,8]{1,0:T(8,128)(4,1)}, pred[512,8]{1,0:T(8,128)(4,1)S(1)}, u32[]{:S(2)}) copy-start(pred[512,8]{1,0:T(8,128)(4,1)S(1)} %get-tuple-element.33) | copy-start | bytes 12292
  43.1 1.3 copy-start.4
  47.9 38.2 %copy-start.10 = (s32[2]{0:T(128)S(1)}, s32[2]{0:T(128)}, u32[]{:S(2)}) copy-start(s32[2]{0:T(128)} %constant.235) | copy-start | bytes 28
  48.0 38.2 %copy-start.9 = (s32[2]{0:T(128)S(1)}, s32[2]{0:T(128)}, u32[]{:S(2)}) copy-start(s32[2]{0:T(128)} %constant.232) | copy-start | bytes 28
  109.7 32.5 %all-to-all-start = ((bf16[64,2,1536]{2,1,0:T(2,128)(2,1)}), bf16[64,2,1536]{2,1,0:T(2,128)(2,1)S(1)}, u32[]{:S(2)}, u32[]{:S(2)}) async-start(bf16[64,2,1536]{2,1,0:T(2,128)(2,1)} %broadcast_select_fusion), calls=%async_computation | async-start | bytes 786432 | tf_op jit(solution)/shard_map/all_to_all | solution.py:47
  121.8 328.0 %all-reduce.3.cloned.1.call-start = ((), (), s32[]{:S(2)}) async-start(), calls=%async_computation.2 | async-start | bytes 2097152 | tf_op jit(solution)/shard_map/psum | solution.py:76
  456.4 1.0 copy-start.3
  469.1 0.6 copy-start.7
  613.3 4.6 copy-start.2
Sparse Core Ops, SparseCore 0:
  190.6 259.1 all-reduce.2
where the time goes:
time: 638 us; the launch traced here: 630 us
  waiting for transfers between devices  249 us (39%)
  other arithmetic  149 us (23%)
  local copies, waits for them, and re-layouts  143 us (22%)
  matrix products  29.9 us (5%)
  blocking collectives  29.8 us (5%)
  between operations  17.2 us (3%)
  starting transfers between devices  12.1 us (2%)
    psum x1, waiting for transfers between devices, shards(): gram_matrix = lax.psum(partial_gram, ('elem', 'snap'))  249 us
    another operation x14, other arithmetic, shards(): lower_factor = jnp.linalg.cholesky(gram_matrix)  80.7 us
    another operation x3, other arithmetic, shards(): jax.scipy.linalg.solve_triangular(lower_factor, identity_matrix, lower=True)  42.6 us
    gather x4, local copies, waits for them, and re-layouts, shards(): peer_ranks = jnp.take_along_axis(ranks_by_owner, owners, axis=1)  35.9 us
    all_to_all x1, blocking collectives, shards(): lax.all_to_all(projected, 'snap', split_axis=1, concat_axis=2, tiled=True)  29.8 us
    gather x3, local copies, waits for them, and re-layouts, shards(): stored_rows = jnp.where(live_nodes, node_slot[jnp.maximum(node_ids, 0)], 0)  24.1 us
    unnamed x28, local copies, waits for them, and re-layouts  21.4 us
    another operation x12, local copies, waits for them, and re-layouts  13.5 us
  transfers between devices with their start and end apart: 2, of which 1 were waited for; matrix products, arithmetic and copies ran while one was open for 5% of the time, Pallas kernels for 0%

commit v1 on v0

--- a/solution.py
+++ b/solution.py
@@ -73,7 +73,7 @@
     partial_gram = lax.dot_general(
         band_rows, band_rows, (((0,), (0,)), ((), ())), preferred_element_type=jnp.float32
     )
-    gram_matrix = lax.psum(partial_gram, ("elem", "snap"))
+    gram_matrix = lax.psum(lax.psum(partial_gram, "elem"), "snap")
     gram_matrix = gram_matrix / total_rows
     lower_factor = jnp.linalg.cholesky(gram_matrix)
     identity_matrix = jnp.eye(columns, dtype=jnp.float32)

time: 638 us -> 618 us (0.969)
  waiting for transfers between devices: 249 us -> 227 us
    psum x1 -> x2, waiting for transfers between devices: 249 us -> 227 us  [shards(): gram_matrix = lax.psum(lax.psum(partial_gram, 'elem'), 'snap')]
  transfers between devices with their start and end apart: 2 -> 3, of which waited for: 1 -> 2; matrix products, arithmetic and copies ran while one was open for 5% -> 5% of each run, Pallas kernels for 0% -> 0%
where the time goes in v1:
time: 618 us; the launch traced here: 609 us
  waiting for transfers between devices  227 us (37%)
  other arithmetic  149 us (24%)
  local copies, waits for them, and re-layouts  143 us (23%)
  matrix products  29.9 us (5%)
  blocking collectives  29.8 us (5%)
  between operations  17.2 us (3%)
  starting transfers between devices  12.2 us (2%)
    psum x2, waiting for transfers between devices, shards(): gram_matrix = lax.psum(lax.psum(partial_gram, 'elem'), 'snap')  227 us
    another operation x14, other arithmetic, shards(): lower_factor = jnp.linalg.cholesky(gram_matrix)  80.7 us
    another operation x3, other arithmetic, shards(): jax.scipy.linalg.solve_triangular(lower_factor, identity_matrix, lower=True)  42.6 us
    gather x4, local copies, waits for them, and re-layouts, shards(): peer_ranks = jnp.take_along_axis(ranks_by_owner, owners, axis=1)  35.9 us
    all_to_all x1, blocking collectives, shards(): lax.all_to_all(projected, 'snap', split_axis=1, concat_axis=2, tiled=True)  29.8 us
    gather x3, local copies, waits for them, and re-layouts, shards(): stored_rows = jnp.where(live_nodes, node_slot[jnp.maximum(node_ids, 0)], 0)  24.1 us
    unnamed x28, local copies, waits for them, and re-layouts  21.4 us
    another operation x12, local copies, waits for them, and re-layouts  13.5 us
  transfers between devices with their start and end apart: 3, of which 2 were waited for; matrix products, arithmetic and copies ran while one was open for 5% of the time, Pallas kernels for 0%

profile of v1, /device:TPU:2, one launch (start us, length us, event | category | flops | bytes accessed | tf_op | source)
XLA Modules:
  0.0 608.7 jit_solution(494993440375793531)
XLA Ops:
  10.3 2.9 gather_fusion
  15.9 23.0 %gather_fusion.2 = s32[4096]{0:T(1024)S(1)} fusion(s32[65536]{0:T(1024)S(1)} %copy-done.1, s32[4096]{0:T(1024)S(1)} %broadcast_clamp_fusion), kind=kCustom, calls=%fused_computation.2 | custom fusion | bytes 49152 | tf_op jit(solution)/shard_map/gather | solution.py:22
  48.0 33.0 %gather_fusion.7 = s32[4096]{0:T(1024)S(1)} fusion(s32[512,64]{0,1:T(8,128)S(1)} %convolution_convert_fusion.2, s32[4096]{0:T(1024)S(1)} %reshape.363), kind=kCustom, calls=%fused_computation.7 | custom fusion | bytes 65536 | tf_op jit(solution)/shard_map/jit(take_along_axis)/gather | solution.py:37
  88.4 15.5 %scatter_custom_fusion.1 = s32[128]{0:T(128)S(1)} fusion(s32[4096]{0:T(1024)S(1)} %reshape.377, s32[4096]{0:T(1024)S(1)} %reshape.379, s32[]{:T(128)} %constant.211.clone.1), kind=kCustom, calls=%fused_computation.155 | custom fusion | bytes 516
  109.7 12.1 %all-to-all-start = ((bf16[64,2,1536]{2,1,0:T(2,128)(2,1)}), bf16[64,2,1536]{2,1,0:T(2,128)(2,1)S(1)}, u32[]{:S(2)}, u32[]{:S(2)}) async-start(bf16[64,2,1536]{2,1,0:T(2,128)(2,1)} %broadcast_select_fusion), calls=%async_computation | async-start | bytes 786432 | tf_op jit(solution)/shard_map/all_to_all | solution.py:47
  124.7 3.2 scatter_custom_fusion
  151.1 29.8 %all_to_all.20 = bf16[16,512,128]{2,0,1:T(8,128)(2,1)} all-to-all(bf16[16,512,128]{2,0,1:T(8,128)(2,1)S(1)} %copy.125), channel_id=1, replica_groups=mesh['elem'=64,'snap'=4] {'snap'}, dimensions={1} | all-to-all | bytes 4194304 | tf_op jit(solution)/shard_map/all_to_all | solution.py:69
  180.9 5.1 copy.126
  186.0 4.5 fusion
  190.6 188.0 %all-reduce.4.cloned.1.call-done = f32[512,512]{0,1:T(8,128)} async-done(((f32[512,512]{0,1:T(8,128)}), f32[512,512]{0,1:T(8,128)}) %all-reduce.4.cloned.1.call-update) | async-done | bytes 1048592 | tf_op jit(solution)/shard_map/psum | solution.py:76
  380.5 4.5 copy.127
  385.1 4.3 dot_general.24
  389.4 39.1 %all-reduce.6.cloned.1.call-done = f32[512,512]{0,1:T(8,128)} async-done(((f32[512,512]{0,1:T(8,128)}), f32[512,512]{0,1:T(8,128)}) %all-reduce.6.cloned.1.call-update) | async-done | bytes 1048592 | tf_op jit(solution)/shard_map/psum | solution.py:76
  436.0 11.7 %cholesky.104 = f32[128,128]{1,0:T(8,128)S(1)} custom-call(f32[128,128]{1,0:T(8,128)S(1)} %cholesky.266), custom_call_target="Cholesky" | custom-call | tf_op jit(solution)/shard_map/jit(cholesky)/cholesky | solution.py:78
  448.4 9.8 %custom-call.31 = f32[1,128,128]{1,2,0:T(8,128)S(1)} custom-call(f32[1,128,128]{2,1,0:T(8,128)S(1)} %get-tuple-element.47), custom_call_target="InvertDiagBlocksLowerTriangular" | custom-call | tf_op jit(solution)/shard_map/jit(cholesky)/cholesky | solution.py:78
  462.6 11.7 %cholesky.217 = f32[128,128]{1,0:T(8,128)S(1)} custom-call(f32[128,128]{1,0:T(8,128)S(1)} %cholesky.270), custom_call_target="Cholesky" | custom-call | tf_op jit(solution)/shard_map/jit(cholesky)/cholesky | solution.py:78
  477.6 10.2 %custom-call.32 = f32[1,128,128]{1,2,0:T(8,128)S(1)} custom-call(f32[1,128,128]{2,1,0:T(8,128)S(1)} %get-tuple-element.44), custom_call_target="InvertDiagBlocksLowerTriangular" | custom-call | tf_op jit(solution)/shard_map/jit(cholesky)/cholesky | solution.py:78
  491.1 11.7 %cholesky.238 = f32[128,128]{1,0:T(8,128)S(1)} custom-call(f32[128,128]{1,0:T(8,128)S(1)} %cholesky.275), custom_call_target="Cholesky" | custom-call | tf_op jit(solution)/shard_map/jit(cholesky)/cholesky | solution.py:78
  504.1 9.8 %custom-call.33 = f32[1,128,128]{1,2,0:T(8,128)S(1)} custom-call(f32[1,128,128]{2,1,0:T(8,128)S(1)} %get-tuple-element.41), custom_call_target="InvertDiagBlocksLowerTriangular" | custom-call | tf_op jit(solution)/shard_map/jit(cholesky)/cholesky | solution.py:78
  516.2 11.9 %cholesky.255 = f32[128,128]{1,0:T(8,128)S(1)} custom-call(f32[128,128]{1,0:T(8,128)S(1)} %convolution_subtract_fusion.5), custom_call_target="Cholesky" | custom-call | tf_op jit(solution)/shard_map/jit(cholesky)/cholesky | solution.py:78
  535.8 13.5 %while.1 = (s32[]{:T(128)}, f32[512,512]{1,0:T(8,128)}, s32[4,2]{0,1:T(2,128)S(1)}, f32[4,128,128]{2,1,0:T(8,128)}, s32[]{:T(128)}) while((s32[]{:T(128)}, f32[512,512]{1,0:T(8,128)}, s32[4,2]{0,1:T(2,128)S(1)}, f32[4,128,128]{2,1,0:T(8,128)}, s32[]{:T(128)}) %tuple.39), condition=%wide.while_cond, body=%wide.while_body.sunk | while | flops 2 | bytes 132205 | solution.py:80
  536.4 2.8 bitcast_dynamic-update-slice_fusion.2
  549.3 40.1 %custom-call.34 = f32[4,128,128]{1,2,0:T(8,128)S(1)} custom-call(f32[4,128,128]{2,1,0:T(8,128)} %get-tuple-element.9), custom_call_target="InvertDiagBlocksLowerTriangular" | custom-call | tf_op jit(solution)/shard_map/jit(_solve_triangular)/triangular_solve | solution.py:80
  596.5 5.1 fusion.4
  (140 shorter events, 101.5 us)
Async XLA Ops:
  7.2 97.9 %copy-start = (bf16[1024,1536]{1,0:T(8,128)(2,1)S(1)}, bf16[1024,1536]{1,0:T(8,128)(2,1)}, u32[]{:S(2)}) copy-start(bf16[1024,1536]{1,0:T(8,128)(2,1)} %param.7) | copy-start | bytes 9437188
  8.0 7.9 %copy-start.1 = (s32[65536]{0:T(1024)S(1)}, s32[65536]{0:T(1024)}, u32[]{:S(2)}) copy-start(s32[65536]{0:T(1024)} %param.12) | copy-start | bytes 786436
  39.0 8.6 %copy-start.8 = (s32[512]{0:T(512)S(1)}, s32[512]{0:T(512)}, u32[]{:S(2)}) copy-start(s32[512]{0:T(512)} %param.13) | copy-start | bytes 6148
  40.0 1.9 copy-start.5
  41.9 40.0 %copy-start.6 = (pred[512,8]{1,0:T(8,128)(4,1)}, pred[512,8]{1,0:T(8,128)(4,1)S(1)}, u32[]{:S(2)}) copy-start(pred[512,8]{1,0:T(8,128)(4,1)S(1)} %get-tuple-element.33) | copy-start | bytes 12292
  43.1 1.3 copy-start.4
  47.9 38.2 %copy-start.10 = (s32[2]{0:T(128)S(1)}, s32[2]{0:T(128)}, u32[]{:S(2)}) copy-start(s32[2]{0:T(128)} %constant.235) | copy-start | bytes 28
  48.0 38.2 %copy-start.9 = (s32[2]{0:T(128)S(1)}, s32[2]{0:T(128)}, u32[]{:S(2)}) copy-start(s32[2]{0:T(128)} %constant.232) | copy-start | bytes 28
  109.7 32.5 %all-to-all-start = ((bf16[64,2,1536]{2,1,0:T(2,128)(2,1)}), bf16[64,2,1536]{2,1,0:T(2,128)(2,1)S(1)}, u32[]{:S(2)}, u32[]{:S(2)}) async-start(bf16[64,2,1536]{2,1,0:T(2,128)(2,1)} %broadcast_select_fusion), calls=%async_computation | async-start | bytes 786432 | tf_op jit(solution)/shard_map/all_to_all | solution.py:47
  121.8 256.7 %all-reduce.4.cloned.1.call-start = ((), (), s32[]{:S(2)}) async-start(), calls=%async_computation.2 | async-start | bytes 2097152 | tf_op jit(solution)/shard_map/psum | solution.py:76
  190.5 237.9 %all-reduce.6.cloned.1.call-start = ((), (), s32[]{:S(2)}) async-start(), calls=%async_computation.3 | async-start | bytes 2097152 | tf_op jit(solution)/shard_map/psum | solution.py:76
  435.1 1.0 copy-start.3
  447.7 0.6 copy-start.7
  591.9 4.6 copy-start.2
Sparse Core Ops, SparseCore 0:
  190.6 187.8 all-reduce.3
  380.9 47.4 all-reduce.5
